TPU v7x, 128 devices: a whole 4x4x4 slice. The times are simulated.
128 devices in a mesh: dp: 8 (over y, core), mp: 16 (over x, z).
Axes of the slice: x: 4, y: 4, z: 4, core: 2. Of those that a mesh axis runs over, the one named last changes fastest.
Arguments:
- tokens: bfloat16 [1024, 8192], P('dp', 'mp'), may hold values from -6 to 6
- grad_out: bfloat16 [1024, 8192], P('dp', 'mp'), may hold values from -6 to 6
- gate_weight: bfloat16 [1024, 128, 128], P('mp'), may hold values from -0.1875 to 0.1875
- up_weight: bfloat16 [1024, 128, 128], P('mp'), may hold values from -0.1875 to 0.1875
- down_weight: bfloat16 [1024, 128, 128], P('mp'), may hold values from -0.125 to 0.125
- gate_block_pairs: int32 [1024, 2], replicated, may hold values from 0 to 111, as said below
- up_blocks: int32 [1024, 2], replicated, may hold values from 0 to 111, as said below
- down_blocks: int32 [1024, 2], replicated, may hold values from 0 to 111, as said below
- column_order: int32 [112], replicated, may hold values from 0 to 111, as said below
Outputs:
- hidden_owned: bfloat16 [1024, 14336], P('dp', 'mp')
- output: bfloat16 [1024, 8192], P('dp', 'mp')
- input_grad: bfloat16 [1024, 8192], P('dp', 'mp')
- gate_grad: bfloat16 [1024, 128, 128], P('mp', 'dp')
- up_grad: bfloat16 [1024, 128, 128], P('mp', 'dp')
- down_grad: bfloat16 [1024, 128, 128], P('mp', 'dp')
Inputs may be any that keep to these rules, and one draw needn't show every extreme that they name: A permutation of the hidden column blocks; index j of mp owns the column blocks column_order[j * 7] to column_order[(j + 1) * 7 - 1]. `gate_block_pairs`: row k holds the row block (of 64) and column block (of 112) of gate block k; no block appears twice; block k = i * 64 + j * 4 + s with 0 <= s < 4 lies in a column block owned by index j; every column block holds at least one block. `up_blocks`: as gate_block_pairs, for the up blocks. `down_blocks`: row k holds the hidden block (of 112) and width block (of 64) of down block k; no block appears twice; block k = i * 64 + j * 4 + s with 0 <= s < 4 lies in a hidden block owned by index j; every hidden block holds at least one block.
All inputs are finite; a program needn't handle non-finite values.
Results may differ from a plain program's by a relative error of at most 0.024.
Values may be sent and summed in bfloat16 or wider, within the bound.
No kernel may reach another device: no remote copies, remote signals or barrier semaphores. Data moves between devices by JAX's collectives and lax.ppermute only.
A program may use at most 128 MiB of HBM per device.

v0:
```python
import jax
import jax.numpy as jnp
from jax import lax
from jax.sharding import PartitionSpec as P


def block_rows(matrix, block_size):
    return matrix.reshape(matrix.shape[0], matrix.shape[1] // block_size, block_size).transpose(
        1, 0, 2
    )


def row_matrix(blocks):
    return blocks.transpose(1, 0, 2).reshape(blocks.shape[1], blocks.shape[0] * blocks.shape[2])


def lookup(lookup_table, indices_in):
    matches = indices_in[:, None] == jnp.arange(lookup_table.shape[0], dtype=jnp.int32)[None, :]
    return jnp.sum(jnp.where(matches, lookup_table[None, :], 0), axis=1)


def segment_total(products, segment_ids, segment_count):
    return jax.ops.segment_sum(products, segment_ids, num_segments=segment_count)


def silu_parts(gate_sum):
    sigmoid = jax.nn.sigmoid(gate_sum)
    return (gate_sum * sigmoid, sigmoid)


def deltas_of(hidden_grad, gate_own, up_own, activated, sigmoid):
    gate_delta = (hidden_grad * up_own * sigmoid * (1.0 + gate_own * (1.0 - sigmoid))).astype(
        jnp.bfloat16
    )
    up_delta = (hidden_grad * activated).astype(jnp.bfloat16)
    return (gate_delta, up_delta)


def body(
    tokens,
    grad_out,
    gate_weight,
    up_weight,
    down_weight,
    gate_block_pairs,
    up_blocks,
    down_blocks,
    column_order,
):
    block_size = gate_weight.shape[1]
    model_groups = lax.axis_size("mp")
    blocks_here = gate_weight.shape[0]
    column_count = column_order.shape[0]
    row_count = tokens.shape[1] * model_groups // block_size
    member = lax.axis_index("mp")
    arange_cols = jnp.arange(column_count, dtype=jnp.int32)
    matches = column_order[None, :] == arange_cols[:, None]
    positions = jnp.sum(jnp.where(matches, arange_cols[None, :], 0), axis=1)
    inputs = lax.all_gather(block_rows(tokens, block_size), "mp", axis=0, tiled=True)
    cotangent = lax.all_gather(block_rows(grad_out, block_size), "mp", axis=0, tiled=True)
    first_block = member * blocks_here
    gate_list = lax.dynamic_slice_in_dim(gate_block_pairs, first_block, blocks_here, 0)
    up_list = lax.dynamic_slice_in_dim(up_blocks, first_block, blocks_here, 0)
    down_list = lax.dynamic_slice_in_dim(down_blocks, first_block, blocks_here, 0)
    gate_pos = lookup(positions, gate_list[:, 1])
    up_pos = lookup(positions, up_list[:, 1])
    down_pos = lookup(positions, down_list[:, 0])
    down_cols = down_list[:, 1]
    gate_inputs = jnp.take(inputs, gate_list[:, 0], axis=0)
    up_inputs = jnp.take(inputs, up_list[:, 0], axis=0)
    gate_part = segment_total(
        jnp.einsum("btk,bkn->btn", gate_inputs, gate_weight, preferred_element_type=jnp.float32),
        gate_pos,
        column_count,
    ).astype(jnp.bfloat16)
    up_part = segment_total(
        jnp.einsum("btk,bkn->btn", up_inputs, up_weight, preferred_element_type=jnp.float32),
        up_pos,
        column_count,
    ).astype(jnp.bfloat16)
    gate_own, up_own = (
        lax.psum_scatter(gate_part, "mp", scatter_dimension=0, tiled=True).astype(jnp.float32),
        lax.psum_scatter(up_part, "mp", scatter_dimension=0, tiled=True).astype(jnp.float32),
    )
    activated, sigmoid = silu_parts(gate_own)
    hidden_own = (activated * up_own).astype(jnp.bfloat16)
    hidden_all = lax.all_gather(hidden_own, "mp", axis=0, tiled=True)
    hidden_taken = jnp.take(hidden_all, down_pos, axis=0)
    output_part = segment_total(
        jnp.einsum("btk,bkn->btn", hidden_taken, down_weight, preferred_element_type=jnp.float32),
        down_cols,
        row_count,
    )
    cot_taken = jnp.take(cotangent, down_cols, axis=0)
    down_local = jnp.einsum(
        "btk,btn->bkn", hidden_taken, cot_taken, preferred_element_type=jnp.float32
    )
    hidden_part = segment_total(
        jnp.einsum("btn,bkn->btk", cot_taken, down_weight, preferred_element_type=jnp.float32),
        down_pos,
        column_count,
    ).astype(jnp.bfloat16)
    hidden_grad = lax.psum_scatter(hidden_part, "mp", scatter_dimension=0, tiled=True).astype(
        jnp.float32
    )
    gate_delta, up_delta = deltas_of(hidden_grad, gate_own, up_own, activated, sigmoid)
    gate_deltas, up_deltas = (
        lax.all_gather(gate_delta, "mp", axis=0, tiled=True),
        lax.all_gather(up_delta, "mp", axis=0, tiled=True),
    )
    gate_taken = jnp.take(gate_deltas, gate_pos, axis=0)
    up_taken = jnp.take(up_deltas, up_pos, axis=0)
    gate_local = jnp.einsum(
        "btk,btn->bkn", gate_inputs, gate_taken, preferred_element_type=jnp.float32
    )
    up_local = jnp.einsum("btk,btn->bkn", up_inputs, up_taken, preferred_element_type=jnp.float32)
    input_part = segment_total(
        jnp.einsum("btn,bkn->btk", gate_taken, gate_weight, preferred_element_type=jnp.float32),
        gate_list[:, 0],
        row_count,
    )
    input_part = input_part + segment_total(
        jnp.einsum("btn,bkn->btk", up_taken, up_weight, preferred_element_type=jnp.float32),
        up_list[:, 0],
        row_count,
    )
    gate_summed, up_summed, down_summed = (
        lax.psum_scatter(
            gate_local.astype(jnp.bfloat16), "dp", scatter_dimension=1, tiled=True
        ).astype(jnp.float32),
        lax.psum_scatter(
            up_local.astype(jnp.bfloat16), "dp", scatter_dimension=1, tiled=True
        ).astype(jnp.float32),
        lax.psum_scatter(
            down_local.astype(jnp.bfloat16), "dp", scatter_dimension=1, tiled=True
        ).astype(jnp.float32),
    )
    gate_grad = gate_summed.astype(jnp.bfloat16)
    up_grad = up_summed.astype(jnp.bfloat16)
    down_grad = down_summed.astype(jnp.bfloat16)
    output = lax.psum_scatter(
        output_part.astype(jnp.bfloat16), "mp", scatter_dimension=0, tiled=True
    )
    input_grad = lax.psum_scatter(
        input_part.astype(jnp.bfloat16), "mp", scatter_dimension=0, tiled=True
    )
    return (
        row_matrix(hidden_own),
        row_matrix(output),
        row_matrix(input_grad),
        gate_grad,
        up_grad,
        down_grad,
    )


def solution(mesh):
    return jax.shard_map(
        body,
        mesh=mesh,
        in_specs=(
            P("dp", "mp"),
            P("dp", "mp"),
            P("mp", None, None),
            P("mp", None, None),
            P("mp", None, None),
            P(),
            P(),
            P(),
            P(),
        ),
        out_specs=(
            P("dp", "mp"),
            P("dp", "mp"),
            P("dp", "mp"),
            P("mp", "dp", None),
            P("mp", "dp", None),
            P("mp", "dp", None),
        ),
        check_vma=False,
    )
```

profile of v0, /device:TPU:0, one launch (start us, length us, event | category | flops | bytes accessed | tf_op | source)
XLA Modules:
  0.0 768.8 jit_solution(10594474711835832623)
XLA Ops:
  14.4 43.8 %all-gather.6.cloned.1.call-done = bf16[64,128,128]{2,1,0:T(8,128)(2,1)} async-done(((bf16[4,128,128]{2,1,0:T(8,128)(2,1)}), bf16[64,128,128]{2,1,0:T(8,128)(2,1)}) %all-gather.6.cloned.1.call-update) | async-done | bytes 2097168 | tf_op jit(solution)/shard_map/all_gather | solution.py:59
  70.9 13.8 %scatter_fusion = f32[112,128,128]{2,1,0:T(8,128)} fusion(f32[112,128,128]{2,1,0:T(8,128)} %broadcast.17.clone.1, s32[64]{0:T(128)S(1)} %get-tuple-element.34, f32[64,128,128]{2,1,0:T(8,128)} %fusion), kind=kCustom, calls=%fused_computation.6 | custom fusion | flops 1048576 | bytes 12583168 | tf_op jit(solution)/shard_map/scatter-add | solution.py:23
  84.7 5.8 convert_element_type.48
  102.7 13.7 %scatter_fusion.1 = f32[112,128,128]{2,1,0:T(8,128)} fusion(f32[112,128,128]{2,1,0:T(8,128)} %broadcast.17.clone.2, s32[64]{0:T(128)S(1)} %get-tuple-element.33, f32[64,128,128]{2,1,0:T(8,128)} %fusion.1), kind=kCustom, calls=%fused_computation.7 | custom fusion | flops 1048576 | bytes 12583168 | tf_op jit(solution)/shard_map/scatter-add | solution.py:23
  116.3 5.9 convert_element_type.50
  126.2 6.0 fusion.3
  136.0 13.7 %scatter_fusion.3 = f32[112,128,128]{2,1,0:T(8,128)} fusion(f32[112,128,128]{2,1,0:T(8,128)} %broadcast.17.clone, s32[64]{0:T(128)S(1)} %get-tuple-element.32, f32[64,128,128]{2,1,0:T(8,128)} %fusion.3), kind=kCustom, calls=%fused_computation.9 | custom fusion | flops 1048576 | bytes 12583168 | tf_op jit(solution)/shard_map/scatter-add | solution.py:23
  149.8 5.9 convert_element_type.54
  155.8 29.7 %reduce-scatter.25.cloned.1.call-done = bf16[7,128,128]{2,1,0:T(8,128)(2,1)} async-done(((bf16[112,128,128]{2,1,0:T(8,128)(2,1)}), bf16[7,128,128]{2,1,0:T(8,128)(2,1)}) %reduce-scatter.25.cloned.1.call-update) | async-done | bytes 229392
  186.5 78.7 %reduce-scatter.27.cloned.1.call-done = bf16[7,128,128]{2,1,0:T(8,128)(2,1)} async-done(((bf16[112,128,128]{2,1,0:T(8,128)(2,1)}), bf16[7,128,128]{2,1,0:T(8,128)(2,1)}) %reduce-scatter.27.cloned.1.call-update) | async-done | bytes 229392
  266.3 78.7 %reduce-scatter.29.cloned.1.call-done = bf16[7,128,128]{2,1,0:T(8,128)(2,1)} async-done(((bf16[112,128,128]{2,1,0:T(8,128)(2,1)}), bf16[7,128,128]{2,1,0:T(8,128)(2,1)}) %reduce-scatter.29.cloned.1.call-update) | async-done | bytes 229392
  349.5 47.1 %all-gather.14.cloned.1.call-done = bf16[112,128,128]{2,1,0:T(8,128)(2,1)} async-done(((bf16[7,128,128]{2,1,0:T(8,128)(2,1)}), bf16[112,128,128]{2,1,0:T(8,128)(2,1)}) %all-gather.14.cloned.1.call-update) | async-done | bytes 3670032 | tf_op jit(solution)/shard_map/all_gather | solution.py:109
  408.3 13.5 %scatter_fusion.5 = f32[64,128,128]{2,1,0:T(8,128)} fusion(f32[64,128,128]{2,1,0:T(8,128)} %broadcast.19.clone.2, s32[64]{0:T(128)S(1)} %get-tuple-element.53, f32[64,128,128]{2,1,0:T(8,128)} %fusion.5), kind=kCustom, calls=%fused_computation.11 | custom fusion | flops 1048576 | bytes 12583168 | tf_op jit(solution)/shard_map/scatter-add | solution.py:23
  421.8 26.2 %all-gather.12.cloned.1.call-done = bf16[112,128,128]{2,1,0:T(8,128)(2,1)} async-done(((bf16[7,128,128]{2,1,0:T(8,128)(2,1)}), bf16[112,128,128]{2,1,0:T(8,128)(2,1)}) %all-gather.12.cloned.1.call-update) | async-done | bytes 3670032 | tf_op jit(solution)/shard_map/all_gather | solution.py:108
  451.0 5.9 fusion.4
  459.4 13.6 %scatter_fusion.4 = f32[64,128,128]{2,1,0:T(8,128)} fusion(f32[64,128,128]{2,1,0:T(8,128)} %broadcast.19.clone.1, s32[64]{0:T(128)S(1)} %get-tuple-element.46, f32[64,128,128]{2,1,0:T(8,128)} %fusion.4), kind=kCustom, calls=%fused_computation.10 | custom fusion | flops 1048576 | bytes 12583168 | tf_op jit(solution)/shard_map/scatter-add | solution.py:23
  473.1 5.8 add_convert_fusion
  478.9 20.6 %all-gather.8.cloned.1.call-done = bf16[112,128,128]{2,1,0:T(8,128)(2,1)} async-done(((bf16[7,128,128]{2,1,0:T(8,128)(2,1)}), bf16[112,128,128]{2,1,0:T(8,128)(2,1)}) %all-gather.8.cloned.1.call-update) | async-done | bytes 3670032 | tf_op jit(solution)/shard_map/all_gather | solution.py:87
  510.0 13.6 %scatter_fusion.2 = f32[64,128,128]{2,1,0:T(8,128)} fusion(f32[64,128,128]{2,1,0:T(8,128)} %broadcast.19.clone, s32[64]{0:T(128)S(1)} %get-tuple-element.48, f32[64,128,128]{2,1,0:T(8,128)} %fusion.2), kind=kCustom, calls=%fused_computation.8 | custom fusion | flops 1048576 | bytes 12583168 | tf_op jit(solution)/shard_map/scatter-add | solution.py:23
  544.3 32.8 %reduce-scatter.17.cloned.1.call-done = bf16[4,128,128]{2,1,0:T(8,128)(2,1)} async-done(((bf16[64,128,128]{2,1,0:T(8,128)(2,1)}), bf16[4,128,128]{2,1,0:T(8,128)(2,1)}) %reduce-scatter.17.cloned.1.call-update) | async-done | bytes 131088 | tf_op jit(solution)/shard_map/reduce_scatter | solution.py:144
  578.9 76.0 %reduce-scatter.15.cloned.1.call-done = bf16[4,128,128]{2,1,0:T(8,128)(2,1)} async-done(((bf16[64,128,128]{2,1,0:T(8,128)(2,1)}), bf16[4,128,128]{2,1,0:T(8,128)(2,1)}) %reduce-scatter.15.cloned.1.call-update) | async-done | bytes 131088 | tf_op jit(solution)/shard_map/reduce_scatter | solution.py:141
  656.7 34.4 %reduce-scatter.19.cloned.1.call-done = bf16[64,16,128]{2,1,0:T(8,128)(2,1)} async-done(((bf16[64,128,128]{2,1,0:T(8,128)(2,1)}), bf16[64,16,128]{2,1,0:T(8,128)(2,1)}) %reduce-scatter.19.cloned.1.call-update) | async-done | bytes 262160 | tf_op jit(solution)/shard_map/reduce_scatter | solution.py:128
  691.1 35.5 %reduce-scatter.21.cloned.1.call-done = bf16[64,16,128]{2,1,0:T(8,128)(2,1)} async-done(((bf16[64,128,128]{2,1,0:T(8,128)(2,1)}), bf16[64,16,128]{2,1,0:T(8,128)(2,1)}) %reduce-scatter.21.cloned.1.call-update) | async-done | bytes 262160 | tf_op jit(solution)/shard_map/reduce_scatter | solution.py:131
  726.6 35.6 %reduce-scatter.23.cloned.1.call-done = bf16[64,16,128]{2,1,0:T(8,128)(2,1)} async-done(((bf16[64,128,128]{2,1,0:T(8,128)(2,1)}), bf16[64,16,128]{2,1,0:T(8,128)(2,1)}) %reduce-scatter.23.cloned.1.call-update) | async-done | bytes 262160 | tf_op jit(solution)/shard_map/reduce_scatter | solution.py:134
  (96 shorter events, 98.4 us)
Async XLA Ops:
  7.2 87.2 %copy-start = (bf16[64,128,128]{2,1,0:T(8,128)(2,1)S(1)}, bf16[64,128,128]{2,1,0:T(8,128)(2,1)}, u32[]{:S(2)}) copy-start(bf16[64,128,128]{2,1,0:T(8,128)(2,1)} %param.16) | copy-start | bytes 6291460
  7.2 51.1 %all-gather.6.cloned.1.call-start = ((), (), s32[]{:S(2)}) async-start(), calls=%async_computation.8 | async-start | bytes 2228224 | tf_op jit(solution)/shard_map/all_gather | solution.py:59
  9.2 113.2 %all-gather.10.cloned.1.call-start = ((), (), s32[]{:S(2)}) async-start(), calls=%async_computation.11 | async-start | bytes 2228224 | tf_op jit(solution)/shard_map/all_gather | solution.py:60
  11.1 174.4 %reduce-scatter.25.cloned.1.call-start = ((), (), s32[]{:S(2)}) async-start(), calls=%async_computation.18 | async-start | bytes 3899392
  90.5 174.7 %reduce-scatter.27.cloned.1.call-start = ((), (), s32[]{:S(2)}) async-start(), calls=%async_computation.19 | async-start | bytes 3899392
  122.3 222.7 %reduce-scatter.29.cloned.1.call-start = ((), (), s32[]{:S(2)}) async-start(), calls=%async_computation.20 | async-start | bytes 3899392
  155.7 240.8 %all-gather.14.cloned.1.call-start = ((), (), s32[]{:S(2)}) async-start(), calls=%async_computation.13 | async-start | bytes 3899392 | tf_op jit(solution)/shard_map/all_gather | solution.py:109
  347.3 100.7 %all-gather.12.cloned.1.call-start = ((), (), s32[]{:S(2)}) async-start(), calls=%async_computation.12 | async-start | bytes 3899392 | tf_op jit(solution)/shard_map/all_gather | solution.py:108
  348.3 151.2 %all-gather.8.cloned.1.call-start = ((), (), s32[]{:S(2)}) async-start(), calls=%async_computation.9 | async-start | bytes 3899392 | tf_op jit(solution)/shard_map/all_gather | solution.py:87
  349.3 227.8 %reduce-scatter.17.cloned.1.call-start = ((), (), s32[]{:S(2)}) async-start(), calls=%async_computation.14 | async-start | bytes 2228224 | tf_op jit(solution)/shard_map/reduce_scatter | solution.py:144
  451.0 6.0 copy-start.4
  478.8 176.1 %reduce-scatter.15.cloned.1.call-start = ((), (), s32[]{:S(2)}) async-start(), calls=%async_computation.10 | async-start | bytes 2228224 | tf_op jit(solution)/shard_map/reduce_scatter | solution.py:141
  502.5 5.1 copy-start.5
  527.6 1.6 copy-start.2
  527.6 163.5 %reduce-scatter.19.cloned.1.call-start = ((), (), s32[]{:S(2)}) async-start(), calls=%async_computation.15 | async-start | bytes 2359296 | tf_op jit(solution)/shard_map/reduce_scatter | solution.py:128
  533.1 1.6 copy-start.3
  533.1 193.5 %reduce-scatter.21.cloned.1.call-start = ((), (), s32[]{:S(2)}) async-start(), calls=%async_computation.16 | async-start | bytes 2359296 | tf_op jit(solution)/shard_map/reduce_scatter | solution.py:131
  538.7 223.5 %reduce-scatter.23.cloned.1.call-start = ((), (), s32[]{:S(2)}) async-start(), calls=%async_computation.17 | async-start | bytes 2359296 | tf_op jit(solution)/shard_map/reduce_scatter | solution.py:134
  538.8 223.5 %copy-start.1 = (bf16[64,128,128]{2,1,0:T(8,128)(2,1)S(1)}, bf16[64,128,128]{2,1,0:T(8,128)(2,1)}, u32[]{:S(2)}) copy-start(bf16[64,128,128]{2,1,0:T(8,128)(2,1)} %param.16) | copy-start | bytes 6291460
Sparse Core Ops, SparseCore 0:
  10.7 47.4 all-gather.5
  61.0 44.2 all-gather.9
  108.6 76.7 reduce-scatter.24
  188.6 76.5 reduce-scatter.26
  268.5 76.5 reduce-scatter.28
  347.7 48.8 all-gather.13
  399.3 48.6 all-gather.11
  450.8 48.6 all-gather.7
  502.8 74.3 reduce-scatter.16
  580.3 74.5 reduce-scatter.14
  657.9 33.1 reduce-scatter.18
  693.9 32.6 reduce-scatter.20
  729.6 32.6 reduce-scatter.22
where the time goes:
time: 771 us; the launch traced here: 769 us
  waiting for transfers between devices  539 us (70%)
  other arithmetic  111 us (14%)
  local copies, waits for them, and re-layouts  59.7 us (8%)
  matrix products  44.3 us (6%)
  between operations  14.1 us (2%)
    unnamed x16, waiting for transfers between devices  187 us
    scatter-add x6, other arithmetic, segment_total(): jax.ops.segment_sum(products, segment_ids, num_segments=segment_count)  81.9 us
    reduce_scatter x1, waiting for transfers between devices, body(): lax.psum_scatter(output_part.astype(jnp.bfloat16), 'mp', scatter_dimensio...  76 us
    all_gather x1, waiting for transfers between devices, body(): lax.all_gather(up_delta, 'mp', axis=0, tiled=True)  47.1 us
    all_gather x1, waiting for transfers between devices, body(): lax.all_gather(block_rows(tokens, block_size), 'mp', axis=0, tiled=True)  43.8 us
    reduce_scatter x1, waiting for transfers between devices, body(): lax.psum_scatter(down_local.astype(jnp.bfloat16), 'dp', scatter_dimension...  35.6 us
    reduce_scatter x1, waiting for transfers between devices, body(): lax.psum_scatter(up_local.astype(jnp.bfloat16), 'dp', scatter_dimension=1...  35.5 us
    reduce_scatter x1, waiting for transfers between devices, body(): lax.psum_scatter(gate_local.astype(jnp.bfloat16), 'dp', scatter_dimension...  34.4 us
  transfers between devices with their start and end apart: 13, of which 12 were waited for; matrix products, arithmetic and copies ran while one was open for 27% of the time, Pallas kernels for 0%

commit v1 on v0

v1 whole, which is shorter than its diff:
```python
import functools

import jax
import jax.numpy as jnp
from jax import lax
from jax.experimental import pallas as pl
from jax.experimental.pallas import tpu as pltpu
from jax.sharding import PartitionSpec as P

BS = 128
STEPS = 8
BF = jnp.bfloat16
F32 = jnp.float32


def dot(a, b):
    return lax.dot_general(a, b, (((1,), (0,)), ((), ())), preferred_element_type=F32)


def dot_t(a, b):
    return lax.dot_general(a, b, (((1,), (1,)), ((), ())), preferred_element_type=F32)


def wide(ref, which, block, per):
    lane = pl.multiple_of((block % per) * BS, BS)
    return ref[block // per, which, :, pl.ds(lane, BS)]


def sums_kernel(rows, cols, x_ref, w_ref, act_ref, own_ref, acc, *, per, quota, owned):
    step = pl.program_id(0)
    group = w_ref.shape[1]

    @pl.when(step == 0)
    def _():
        acc[...] = jnp.zeros_like(acc)

    for b in range(group):
        proj = (b // quota) % 3
        r = rows[step * group + b]
        c = cols[step * group + b]
        w = w_ref[:, b].reshape(BS, BS)
        if proj < 2:
            acc[proj, c] += dot(wide(x_ref, 0, r, per), w)
        else:
            acc[proj, c] += dot_t(wide(x_ref, 1, r, per), w)

    @pl.when(step == pl.num_programs(0) - 1)
    def _():
        for c in range(owned):
            gate, up, grad = acc[0, c], acc[1, c], acc[2, c]
            s = jax.nn.sigmoid(gate)
            silu = gate * s
            hidden = (silu * up).astype(BF)
            act_ref[0, c] = hidden
            own_ref[:, c * BS : (c + 1) * BS] = hidden
            act_ref[1, c] = (grad * up * s * (1.0 + gate * (1.0 - s))).astype(BF)
            act_ref[2, c] = (grad * silu).astype(BF)


def parts_kernel(rows, cols, act_ref, w_ref, out_ref, acc, *, per, quota):
    step = pl.program_id(0)
    group = w_ref.shape[1]

    @pl.when(step == 0)
    def _():
        acc[...] = jnp.zeros_like(acc)

    for b in range(group):
        proj = (b // quota) % 3
        r = rows[step * group + b]
        c = cols[step * group + b]
        w = w_ref[:, b].reshape(BS, BS)
        if proj < 2:
            acc[1, r] += dot_t(act_ref[1 + proj, c], w)
        else:
            acc[0, r] += dot(act_ref[0, c], w)

    @pl.when(step == pl.num_programs(0) - 1)
    def _():
        def store(dest, carry):
            for which in range(2):
                for q in range(per):
                    out_ref[dest, which, :, q * BS : (q + 1) * BS] = acc[
                        which, dest * per + q
                    ].astype(BF)
            return carry

        lax.fori_loop(0, out_ref.shape[0], store, 0)


def grads_kernel(rows, cols, xt_ref, x_ref, act_ref, out_ref, ht, *, per, quota):
    step = pl.program_id(0)
    group = out_ref.shape[1]

    @pl.when(step == 0)
    def _():
        for c in range(ht.shape[0]):
            ht[c] = act_ref[0, c].T

    for b in range(group):
        proj = (b // quota) % 3
        r = rows[step * group + b]
        c = cols[step * group + b]
        if proj < 2:
            g = dot(xt_ref[r], act_ref[1 + proj, c])
        else:
            g = dot(ht[c], wide(x_ref, 1, r, per))
        out_ref[:, b] = g.astype(BF).reshape(out_ref.shape[0], -1, BS)


def flip_kernel(x_ref, out_ref, *, per):
    for q in range(per):
        out_ref[q] = x_ref[0, 0, :, q * BS : (q + 1) * BS].T


def full(shape):
    return pl.BlockSpec(shape, lambda *a: (0,) * len(shape))


def body(
    tokens,
    grad_out,
    gate_weight,
    up_weight,
    down_weight,
    gate_block_pairs,
    up_blocks,
    down_blocks,
    column_order,
):
    n_mp, n_dp = lax.axis_size("mp"), lax.axis_size("dp")
    member, shard = lax.axis_index("mp"), lax.axis_index("dp")
    held = gate_weight.shape[0]
    quota = held // n_mp
    slab = BS // n_dp
    per = tokens.shape[1] // BS
    n_rows = per * n_mp
    owned = column_order.shape[0] // n_mp
    total = 3 * held
    group = total // STEPS
    tok = tokens.shape[0]

    x_all = lax.all_gather(jnp.stack([tokens, grad_out]), "mp", axis=0, tiled=False)

    slabs = jnp.stack(
        [
            lax.dynamic_slice_in_dim(w, shard * slab, slab, 1).reshape(n_mp, quota, slab, BS)
            for w in (gate_weight, up_weight, down_weight)
        ],
        axis=1,
    )
    mine = lax.all_to_all(slabs, "mp", split_axis=0, concat_axis=0, tiled=True)
    weights = lax.all_gather(mine.reshape(total, slab, BS), "dp", axis=0, tiled=False)

    tables = jnp.stack([gate_block_pairs, up_blocks, down_blocks[:, ::-1]])
    tables = tables.reshape(3, n_mp, n_mp, quota, 2)
    tables = lax.dynamic_index_in_dim(tables, member, 2, keepdims=False)
    tables = tables.transpose(1, 0, 2, 3).reshape(total, 2)
    own_cols = lax.dynamic_slice_in_dim(column_order, member * owned, owned, 0)
    rows = tables[:, 0]
    cols = jnp.sum(
        jnp.where(
            tables[:, 1][:, None] == own_cols[None, :], jnp.arange(owned, dtype=jnp.int32), 0
        ),
        axis=1,
    )

    x_spec = full(x_all.shape)
    w_spec = pl.BlockSpec((n_dp, group, slab, BS), lambda g, *_: (0, g, 0, 0))
    act_shape = (3, owned, tok, BS)
    params = pltpu.CompilerParams(dimension_semantics=("arbitrary",))

    x_t = pl.pallas_call(
        functools.partial(flip_kernel, per=per),
        out_shape=jax.ShapeDtypeStruct((n_rows, BS, tok), BF),
        grid=(n_mp,),
        in_specs=[pl.BlockSpec((1, 1, tok, per * BS), lambda g: (g, 0, 0, 0))],
        out_specs=pl.BlockSpec((per, BS, tok), lambda g: (g, 0, 0)),
        compiler_params=params,
        name="flip",
    )(x_all)

    act, hidden_own = pl.pallas_call(
        functools.partial(sums_kernel, per=per, quota=quota, owned=owned),
        out_shape=(
            jax.ShapeDtypeStruct(act_shape, BF),
            jax.ShapeDtypeStruct((tok, owned * BS), BF),
        ),
        grid_spec=pltpu.PrefetchScalarGridSpec(
            num_scalar_prefetch=2,
            grid=(STEPS,),
            in_specs=[x_spec, w_spec],
            out_specs=[full(act_shape), full((tok, owned * BS))],
            scratch_shapes=[pltpu.VMEM(act_shape, F32)],
        ),
        compiler_params=params,
        name="sums",
    )(rows, cols, x_all, weights)

    grads = pl.pallas_call(
        functools.partial(grads_kernel, per=per, quota=quota),
        out_shape=jax.ShapeDtypeStruct((n_dp, total, slab, BS), BF),
        grid_spec=pltpu.PrefetchScalarGridSpec(
            num_scalar_prefetch=2,
            grid=(STEPS,),
            in_specs=[full(x_t.shape), x_spec, full(act_shape)],
            out_specs=w_spec,
            scratch_shapes=[pltpu.VMEM((owned, BS, tok), BF)],
        ),
        compiler_params=params,
        name="grads",
    )(rows, cols, x_t, x_all, act)
    grads = lax.psum_scatter(grads, "dp", scatter_dimension=0, tiled=True)

    parts = pl.pallas_call(
        functools.partial(parts_kernel, per=per, quota=quota),
        out_shape=jax.ShapeDtypeStruct((n_mp, 2, tok, per * BS), BF),
        grid_spec=pltpu.PrefetchScalarGridSpec(
            num_scalar_prefetch=2,
            grid=(STEPS,),
            in_specs=[full(act_shape), w_spec],
            out_specs=full((n_mp, 2, tok, per * BS)),
            scratch_shapes=[pltpu.VMEM((2, n_rows, tok, BS), F32)],
        ),
        compiler_params=params,
        name="parts",
    )(rows, cols, act, weights)
    parts = lax.all_to_all(parts, "mp", split_axis=0, concat_axis=0, tiled=True)
    output = jnp.sum(parts[:, 0].astype(F32), axis=0).astype(BF)
    input_grad = jnp.sum(parts[:, 1].astype(F32), axis=0).astype(BF)

    grads = grads.reshape(n_mp, 3, quota, slab, BS)
    grads = lax.all_to_all(grads, "mp", split_axis=0, concat_axis=0, tiled=True)
    gate_grad, up_grad, down_grad = (
        grads[:, p].reshape(held, slab, BS) for p in range(3)
    )
    return (hidden_own, output, input_grad, gate_grad, up_grad, down_grad)


def solution(mesh):
    return jax.shard_map(
        body,
        mesh=mesh,
        in_specs=(
            P("dp", "mp"),
            P("dp", "mp"),
            P("mp", None, None),
            P("mp", None, None),
            P("mp", None, None),
            P(),
            P(),
            P(),
            P(),
        ),
        out_specs=(
            P("dp", "mp"),
            P("dp", "mp"),
            P("dp", "mp"),
            P("mp", "dp", None),
            P("mp", "dp", None),
            P("mp", "dp", None),
        ),
        check_vma=False,
    )
```

time: 771 us -> 224 us (0.29)
  waiting for transfers between devices: 539 us -> 69.9 us
  other arithmetic: 111 us -> 6.45 us
  blocking collectives: 0 us -> 82 us
  local copies, waits for them, and re-layouts: 59.7 us -> 5.58 us
  matrix products: 44.3 us -> 0 us
  Pallas kernels: 0 us -> 41.4 us
    reduce_scatter x5 -> x1, waiting for transfers between devices: 214 us -> 0.01 us  [body(): grads = lax.psum_scatter(grads, 'dp', scatter_dimension=0, tiled=True)]
    unnamed x16 -> x3, waiting for transfers between devices: 187 us -> 0.05 us
    all_to_all x0 -> x2, blocking collectives: none -> 82 us  [the longest x1 58.3 us: body(): parts = lax.all_to_all(parts, 'mp', split_axis=0, concat_axis=0, tiled=True)]
    scatter-add x6 -> x0, other arithmetic: 81.9 us -> none  [segment_total(): jax.ops.segment_sum(products, segment_ids, num_segments=segment_count)]
    all_gather x5 -> x2, waiting for transfers between devices: 138 us -> 60.2 us  [the longest x1 32.2 us: body(): lax.all_gather(mine.reshape(total, slab, BS), 'dp', axis=0, tiled=False)]
    dot_general x9 -> x0, matrix products: 44.3 us -> none  [the longest x1 5.97 us: body(): jnp.einsum('btn,bkn->btk', cot_taken, down_weight, preferred_element_type...]
    pallas_call x0 -> x4, Pallas kernels: none -> 41.4 us  [the longest x1 11.7 us: body(): pl.pallas_call(functools.partial(parts_kernel, per=per, quota=quota), out...]
    convert_element_type x6 -> x0, other arithmetic: 27.7 us -> none  [the longest x1 5.92 us: body(): up_part = segment_total(jnp.einsum('btk,bkn->btn', up_inputs, up_weight,...]
  transfers between devices with their start and end apart: 13 -> 4, of which waited for: 12 -> 3; matrix products, arithmetic and copies ran while one was open for 27% -> 4% of each run, Pallas kernels for 0% -> 10%
where the time goes in v1:
time: 224 us; the launch traced here: 223 us
  blocking collectives  82 us (37%)
  waiting for transfers between devices  69.9 us (31%)
  Pallas kernels  41.4 us (18%)
  between operations  13.9 us (6%)
  other arithmetic  6.45 us (3%)
  local copies, waits for them, and re-layouts  5.58 us (2%)
  starting transfers between devices  3.74 us (2%)
    all_to_all x1, blocking collectives, body(): parts = lax.all_to_all(parts, 'mp', split_axis=0, concat_axis=0, tiled=True)  58.3 us
    all_gather x1, waiting for transfers between devices, body(): lax.all_gather(mine.reshape(total, slab, BS), 'dp', axis=0, tiled=False)  32.2 us
    all_gather x1, waiting for transfers between devices, body(): lax.all_gather(jnp.stack([tokens, grad_out]), 'mp', axis=0, tiled=False)  28 us
    all_to_all x1, blocking collectives, body(): mine = lax.all_to_all(slabs, 'mp', split_axis=0, concat_axis=0, tiled=True)  23.8 us
    pallas_call x1, Pallas kernels, body(): pl.pallas_call(functools.partial(parts_kernel, per=per, quota=quota), out...  11.7 us
    pallas_call x1, Pallas kernels, body(): pl.pallas_call(functools.partial(sums_kernel, per=per, quota=quota, owned...  10.5 us
    pallas_call x1, Pallas kernels, body(): pl.pallas_call(functools.partial(flip_kernel, per=per), out_shape=jax.Sha...  9.91 us
    all_to_all x1, waiting for transfers between devices, body(): grads = lax.all_to_all(grads, 'mp', split_axis=0, concat_axis=0, tiled=True)  9.65 us
  transfers between devices with their start and end apart: 4, of which 3 were waited for; matrix products, arithmetic and copies ran while one was open for 4% of the time, Pallas kernels for 10%

profile of v1, /device:TPU:0, one launch (start us, length us, event | category | flops | bytes accessed | tf_op | source)
XLA Modules:
  0.0 223.1 jit_solution(2933566161194016296)
XLA Ops:
  7.2 1.8 pad_maximum_fusion.1
  9.2 1.1 constant_dynamic-slice_fusion
  10.4 23.8 %all_to_all.15 = bf16[16,3,4,16,128]{4,3,2,1,0:T(8,128)(2,1)} all-to-all(bf16[16,3,4,16,128]{4,3,2,1,0:T(8,128)(2,1)S(1)} %pad_maximum_fusion), channel_id=1, replica_groups=mesh['dp'=8,'mp'=16] {'mp'}, dimensions={0} | all-to-all | bytes 1572864 | tf_op jit(solution)/shard_map/all_to_all | solution.py:152
  34.3 0.2 rev.3
  34.5 0.3 stack.26
  34.8 0.3 copy.24
  35.1 0.3 stack.25
  35.4 0.3 copy.23
  35.7 0.3 stack.24
  36.0 0.3 copy.22
  36.4 0.9 copy.27
  37.5 0.6 fusion.1
  38.0 0.6 select_reduce_fusion.cols
  38.7 28.0 %all-gather.6.cloned.1.call-done = bf16[32,128,512]{2,1,0:T(8,128)(2,1)} async-done(((bf16[2,128,512]{2,1,0:T(8,128)(2,1)}), bf16[32,128,512]{2,1,0:T(8,128)(2,1)}) %all-gather.6.cloned.1.call-update) | async-done | bytes 4194320 | tf_op jit(solution)/shard_map/all_gather | solution.py:143
  66.7 9.9 %flip.1.xt_ref = bf16[64,128,128]{2,1,0:T(8,128)(2,1)} custom-call(bf16[16,2,128,512]{3,2,1,0:T(8,128)(2,1)} %bitcast.24), custom_call_target="tpu_custom_call" | custom-call | tf_op jit(solution)/shard_map/flip/pallas_call | solution.py:173
  76.6 32.2 %all-gather.4.cloned.1.call-done.w_ref = bf16[8,192,16,128]{3,2,1,0:T(8,128)(2,1)} async-done(((bf16[1,192,16,128]{3,2,1,0:T(8,128)(2,1)}), bf16[8,192,16,128]{3,2,1,0:T(8,128)(2,1)}) %all-gather.4.cloned.1.call-update) | async-done | bytes 6291472 | tf_op jit(solution)/shard_map/all_gather | solution.py:153
  108.8 10.5 %sums.1 = (bf16[3,7,128,128]{3,2,1,0:T(8,128)(2,1)}, bf16[128,896]{1,0:T(8,128)(2,1)}) custom-call(s32[192]{0:T(256)} %bitcast.38, s32[192]{0:T(256)} %select_reduce_fusion.cols, bf16[16,2,128,512]{3,2,1,0:T(8,128)(2,1)} %bitcast.25, bf16[8,192,16,128]{3,2,1,0:T(8,128)(2,1)} %all-gather.4.cloned.1.call-done.w_ref), custom_call_target="tpu_custom_call" | custom-call | tf_op jit(solution)/shard_map/sums/pallas_call | solution.py:183
  119.3 9.3 %grads.1 = bf16[8,192,16,128]{3,2,1,0:T(8,128)(2,1)} custom-call(s32[192]{0:T(256)} %bitcast.39, s32[192]{0:T(256)} %select_reduce_fusion.cols, bf16[64,128,128]{2,1,0:T(8,128)(2,1)} %flip.1.xt_ref, bf16[16,2,128,512]{3,2,1,0:T(8,128)(2,1)} %bitcast.26, bf16[3,7,128,128]{3,2,1,0:T(8,128)(2,1)} %get-tuple-element.9.act_ref), custom_call_target="tpu_custom_call" | custom-call | tf_op jit(solution)/shard_map/grads/pallas_call | solution.py:200
  128.6 11.7 %parts.1 = bf16[16,2,128,512]{3,2,1,0:T(8,128)(2,1)} custom-call(s32[192]{0:T(256)} %bitcast.40, s32[192]{0:T(256)} %select_reduce_fusion.cols, bf16[3,7,128,128]{3,2,1,0:T(8,128)(2,1)} %get-tuple-element.9.act_ref, bf16[8,192,16,128]{3,2,1,0:T(8,128)(2,1)} %all-gather.4.cloned.1.call-done.w_ref), custom_call_target="tpu_custom_call" | custom-call | tf_op jit(solution)/shard_map/parts/pallas_call | solution.py:215
  140.4 58.3 %all_to_all.16 = bf16[16,2,128,512]{3,2,1,0:T(8,128)(2,1)} all-to-all(bf16[16,2,128,512]{3,2,1,0:T(8,128)(2,1)} %parts.1), channel_id=1, replica_groups=mesh['dp'=8,'mp'=16] {'mp'}, dimensions={0} | all-to-all | bytes 8388608 | tf_op jit(solution)/shard_map/all_to_all | solution.py:228
  198.6 3.6 %all-to-all-start.2 = ((bf16[16,3,4,16,128]{4,3,2,1,0:T(8,128)(2,1)}), bf16[16,3,4,16,128]{4,3,2,1,0:T(8,128)(2,1)S(1)}, u32[]{:S(2)}, u32[]{:S(2)}) async-start(bf16[16,3,4,16,128]{4,3,2,1,0:T(8,128)(2,1)} %bitcast.31), calls=%async_computation.3 | async-start | bytes 1572864 | tf_op jit(solution)/shard_map/all_to_all | solution.py:233
  202.3 3.8 %slice_reduce_fusion = (bf16[128,512]{1,0:T(8,128)(2,1)}, bf16[128,512]{1,0:T(8,128)(2,1)}) fusion(bf16[16,2,128,512]{3,2,1,0:T(8,128)(2,1)} %all_to_all.16), kind=kLoop, calls=%fused_computation | loop fusion | flops 1966080 | bytes 4456448 | tf_op jit(solution)/shard_map/reduce_sum | solution.py:230
  206.0 9.7 %all-to-all-done.2 = bf16[16,3,4,16,128]{4,3,2,1,0:T(8,128)(2,1)S(1)} async-done(((bf16[16,3,4,16,128]{4,3,2,1,0:T(8,128)(2,1)}), bf16[16,3,4,16,128]{4,3,2,1,0:T(8,128)(2,1)S(1)}, u32[]{:S(2)}, u32[]{:S(2)}) %all-to-all-start.2) | async-done | bytes 786464 | tf_op jit(solution)/shard_map/all_to_all | solution.py:233
  215.7 0.9 fusion
  (22 shorter events, 0.7 us)
Async XLA Ops:
  7.2 2.0 copy-start
  7.2 59.5 %all-gather.6.cloned.1.call-start = ((), (), s32[]{:S(2)}) async-start(), calls=%async_computation.6 | async-start | bytes 4456448 | tf_op jit(solution)/shard_map/all_gather | solution.py:143
  9.1 99.7 %all-gather.4.cloned.1.call-start = ((), (), s32[]{:S(2)}) async-start(), calls=%async_computation.4 | async-start | bytes 7077888 | tf_op jit(solution)/shard_map/all_gather | solution.py:153
  10.3 24.0 %copy-start.3 = (s32[1024,2]{0,1:T(2,128)S(1)}, s32[1024,2]{0,1:T(2,128)}, u32[]{:S(2)}) copy-start(s32[1024,2]{0,1:T(2,128)} %param.16) | copy-start | bytes 24580
  10.3 24.8 %copy-start.1 = (s32[1024,2]{0,1:T(2,128)S(1)}, s32[1024,2]{0,1:T(2,128)}, u32[]{:S(2)}) copy-start(s32[1024,2]{0,1:T(2,128)} %param.15) | copy-start | bytes 24580
  10.4 25.3 %copy-start.2 = (s32[1024,2]{0,1:T(2,128)S(1)}, s32[1024,2]{0,1:T(2,128)}, u32[]{:S(2)}) copy-start(s32[1024,2]{0,1:T(2,128)} %param.14) | copy-start | bytes 24580
  10.4 26.9 %copy-start.4 = (s32[112]{0:T(128)S(1)}, s32[112]{0:T(128)}, u32[]{:S(2)}) copy-start(s32[112]{0:T(128)} %param.17) | copy-start | bytes 1348
  34.2 164.4 %reduce-scatter.2.cloned.1.call-start = ((), (), s32[]{:S(2)}) async-start(), calls=%async_computation.5 | async-start | bytes 7077888 | tf_op jit(solution)/shard_map/reduce_scatter | solution.py:213
  198.6 17.0 %all-to-all-start.2 = ((bf16[16,3,4,16,128]{4,3,2,1,0:T(8,128)(2,1)}), bf16[16,3,4,16,128]{4,3,2,1,0:T(8,128)(2,1)S(1)}, u32[]{:S(2)}, u32[]{:S(2)}) async-start(bf16[16,3,4,16,128]{4,3,2,1,0:T(8,128)(2,1)} %bitcast.31), calls=%async_computation.3 | async-start | bytes 1572864 | tf_op jit(solution)/shard_map/all_to_all | solution.py:233
Sparse Core Ops, SparseCore 0:
  10.7 55.9 all-gather.5
  68.4 40.4 all-gather.3
  128.8 43.0 reduce-scatter.1
